TPU v7x, 32 devices: a whole 2x2x4 slice. The times are simulated.
32 devices in a mesh: groups: 2 (over y), img: 4 (over z), ref: 2 (over x), rep: 2 (over core).
Axes of the slice: x: 2, y: 2, z: 4, core: 2. Of those that a mesh axis runs over, the one named last changes fastest.
Arguments:
- images: float32 [768, 4096], P(('groups', 'img')), parts along dimension 0, may hold values from -24 to 24
- references: float32 [4096, 2048], P('img', ('groups', 'ref', 'rep')), parts along dimension 1, may hold values from -1.2 to 1.2
- rotations: int32 [2048], P(('groups', 'ref', 'rep')), parts along dimension 0, may hold values from 0 to 7
- image_group: int32 [768], P(('groups', 'img')), parts along dimension 0, may hold values from 0 to 15
- noise_var: float32 [16], replicated, may hold values from 0.5 to 2
Outputs:
- class_means: float32 [4096, 2048], P('img', ('groups', 'ref', 'rep')), parts along dimension 1
- class_weights: float32 [2048], P(('groups', 'ref', 'rep')), parts along dimension 0
- log_evidence: float32 [768], P(('groups', 'img')), parts along dimension 0
There are 2 independent parts, one for each index of `groups`. A program takes and returns all parts, laid end to end along the dimension named above; an argument that names none is the same for every part. Nothing has to cross between parts.
All inputs are finite; a program needn't handle non-finite values.
Results may differ from a plain program's by a relative error of at most 0.0003.
Values sent between devices are 32-bit elements; how exact they have to be, the bound alone decides.
A program may use at most 64 MiB of HBM per device.

v0:
```python
import jax
import jax.numpy as jnp
from jax import lax
from jax.sharding import PartitionSpec as P

IMAGE_SIDE = 64
PIXELS = 4096


def joined(part, axis, combine):
    gathered = jax.tree.map(lambda a: lax.all_gather(a, axis), part)

    def take(source):
        return jax.tree.map(lambda a: lax.dynamic_index_in_dim(a, source, 0, False), gathered)

    return lax.fori_loop(
        1, lax.axis_size(axis), lambda source, state: combine(state, take(source)), take(0)
    )


def turn_forward(field, which):
    quarter = which % 4
    base = field if which < 4 else jnp.swapaxes(field, 0, 1)
    return jnp.rot90(base, quarter, axes=(0, 1))


def turn_inverse(field, which):
    quarter = which % 4
    base = jnp.rot90(field, -quarter, axes=(0, 1))
    return base if which < 4 else jnp.swapaxes(base, 0, 1)


def select_turn(field, rotations, turner):
    result = jnp.zeros_like(field)
    for which in range(8):
        result = jnp.where(rotations[None, None, :] == which, turner(field, which), result)
    return result


def combine_stats(first, second):
    top = jnp.maximum(first[0], second[0])
    total = first[1] * jnp.exp(first[0] - top) + second[1] * jnp.exp(second[0] - top)
    return (top, total)


def body(images, references, rotations, image_group, noise_var):
    gathered = lax.all_gather(references, "img", axis=0, tiled=True)
    rotated = select_turn(
        gathered.reshape(IMAGE_SIDE, IMAGE_SIDE, -1), rotations, turn_inverse
    ).reshape(PIXELS, -1)
    norms = jnp.sum(gathered * gathered, axis=0)
    group_hot = image_group[:, None] == jnp.arange(noise_var.shape[0])[None, :]
    sigma = jnp.sum(jnp.where(group_hot, noise_var[None, :], 0.0), axis=1)
    scores = (
        jnp.dot(
            images, rotated, precision=lax.Precision.HIGHEST, preferred_element_type=jnp.float32
        )
        - 0.5 * norms[None, :]
    ) / sigma[:, None]
    local_top = jnp.max(scores, axis=1)
    local_total = jnp.sum(jnp.exp(scores - local_top[:, None]), axis=1)
    top, total = joined((local_top, local_total), ("ref", "rep"), combine_stats)
    log_evidence = top + jnp.log(total)
    posterior = jnp.exp(scores - log_evidence[:, None])
    weight_sum = lax.psum(jnp.sum(posterior, axis=0), "img")
    numer_image = lax.dot_general(
        images,
        posterior,
        (((0,), (0,)), ((), ())),
        precision=lax.Precision.HIGHEST,
        preferred_element_type=jnp.float32,
    )
    numerator = select_turn(
        numer_image.reshape(IMAGE_SIDE, IMAGE_SIDE, -1), rotations, turn_forward
    ).reshape(PIXELS, -1)
    owned = lax.psum_scatter(numerator, "img", scatter_dimension=0, tiled=True)
    class_means = owned / (weight_sum + 1.0)[None, :]
    class_total = weight_sum.shape[0] * lax.axis_size("ref") * lax.axis_size("rep")
    image_total = images.shape[0] * lax.axis_size("img")
    class_weights = weight_sum * (class_total / image_total)
    return (class_means, class_weights, log_evidence)


def solution(mesh):
    placed = (
        P(("groups", "img"), None),
        P("img", ("groups", "ref", "rep")),
        P(("groups", "ref", "rep")),
        P(("groups", "img")),
        P(),
    )
    return jax.shard_map(
        body,
        mesh=mesh,
        in_specs=placed,
        out_specs=(
            P("img", ("groups", "ref", "rep")),
            P(("groups", "ref", "rep")),
            P(("groups", "img")),
        ),
        check_vma=False,
    )
```

profile of v0, /device:TPU:0, one launch (start us, length us, event | category | flops | bytes accessed | tf_op | source)
XLA Modules:
  0.0 286.7 jit_solution(2013551750306974672)
XLA Ops:
  7.2 0.7 all-gather.4.cloned.1.call-update
  8.0 1.2 dynamic-slice
  9.9 0.8 select_reduce_fusion
  10.6 0.7 broadcast_compare_fusion.7
  11.3 81.7 %all-gather.4.cloned.1.call-done = f32[4096,256]{1,0:T(8,128)} async-done(((f32[1024,256]{1,0:T(8,128)}), f32[4096,256]{1,0:T(8,128)}) %all-gather.4.cloned.1.call-update) | async-done | bytes 4194320 | tf_op jit(solution)/shard_map/all_gather | solution.py:47
  93.1 6.6 %rev.41 = f32[64,64,256]{2,1,0:T(8,128)} reverse(f32[64,64,256]{2,1,0:T(8,128)} %bitcast.41), dimensions={0,1} | reverse | bytes 8388608 | tf_op jit(solution)/shard_map/jit(rot90)/jit(_flip)/rev | solution.py:29
  99.7 6.7 %rev.40 = f32[64,64,256]{2,1,0:T(8,128)} reverse(f32[64,64,256]{2,1,0:T(8,128)} %bitcast.42), dimensions={1} | reverse | bytes 8388608 | tf_op jit(solution)/shard_map/jit(rot90)/jit(_flip)/rev | solution.py:29
  106.4 4.7 %rev.42 = f32[64,64,256]{2,0,1:T(8,128)} reverse(f32[64,64,256]{2,0,1:T(8,128)} %bitcast.43), dimensions={1} | reverse | bytes 8388608 | tf_op jit(solution)/shard_map/jit(rot90)/jit(_flip)/rev | solution.py:29
  111.0 2.9 %multiply_reduce_fusion = f32[256]{0:T(256)S(1)} fusion(f32[4096,256]{1,0:T(8,128)} %all-gather.4.cloned.1.call-done), kind=kLoop, calls=%fused_computation.22 | loop fusion | flops 2096896 | bytes 4195328 | tf_op jit(solution)/shard_map/reduce_sum | solution.py:51
  114.5 16.2 %fusion.3 = f32[64,64,256]{2,1,0:T(8,128)S(1)} fusion(f32[64,64,256]{2,1,0:T(8,128)} %rev.40, f32[64,64,256]{2,0,1:T(8,128)} %rev.42, f32[64,64,256]{2,0,1:T(8,128)} %bitcast.52, f32[64,64,256]{2,0,1:T(8,128)S(1)} %bitcast.45, f32[64,64,256]{2,0,1:T(8,128)} %bitcast.53, f32[64,64,256]{2,1,0:T(8,128)} %rev.41, f32[64,64,256]{2,1,0:T(8,128)S(1)} %bitcast.44, ...), kind=kLoop, calls=%fused_computation.9 | loop fusion | flops 8388608 | bytes 33556480 | tf_op jit(solution)/shard_map/jit(_where)/select_n | solution.py:36
  130.7 2.6 fusion.13
  133.9 6.6 %all-reduce.2 = (f32[384]{0:T(512)S(1)}, f32[384]{0:T(512)S(1)}) all-reduce(f32[384]{0:T(512)S(1)} %dynamic-update-slice, f32[384]{0:T(512)S(1)} %dynamic-update-slice.1), channel_id=2, replica_groups=mesh['groups'=2,'img'=4,'ref'=2,'rep'=2] {'ref','rep'}, use_global_device_ids=true, to_apply=%add | all-reduce | flops 768 | bytes 6144
  140.8 5.3 %convolution_bitcast_fusion = f32[4096,256]{0,1:T(8,128)} fusion(f32[96,4096]{1,0:T(8,128)S(1)} %copy-done, f32[256,96]{0,1:T(8,128)S(1)} %get-tuple-element.163, f32[96]{0:T(128)S(1)} %log_add_fusion), kind=kOutput, calls=%fused_computation.6 | convolution fusion | flops 1207984128 | bytes 5865856 | tf_op jit(solution)/shard_map/dot_general | solution.py:66
  146.1 5.6 %copy.31 = f32[4096,256]{1,0:T(8,128)} copy(f32[4096,256]{0,1:T(8,128)} %convolution_bitcast_fusion) | data formatting | bytes 8388608 | tf_op jit(solution)/shard_map/dot_general | solution.py:66
  151.7 6.6 %copy.64 = f32[64,64,256]{2,0,1:T(8,128)} copy(f32[64,64,256]{2,1,0:T(8,128)} %bitcast.46) | data formatting | bytes 8388608 | tf_op jit(solution)/shard_map/reshape | solution.py:74
  158.2 6.7 %rev.45 = f32[64,64,256]{2,1,0:T(8,128)} reverse(f32[64,64,256]{2,1,0:T(8,128)} %bitcast.54), dimensions={1} | reverse | bytes 8388608 | tf_op jit(solution)/shard_map/jit(rot90)/jit(_flip)/rev | solution.py:24
  164.9 6.7 %rev.44 = f32[64,64,256]{2,1,0:T(8,128)} reverse(f32[64,64,256]{2,1,0:T(8,128)} %bitcast.55), dimensions={0,1} | reverse | bytes 8388608 | tf_op jit(solution)/shard_map/jit(rot90)/jit(_flip)/rev | solution.py:24
  171.6 6.6 %rev.43 = f32[64,64,256]{2,1,0:T(8,128)} reverse(f32[64,64,256]{2,1,0:T(8,128)} %bitcast.47), dimensions={1} | reverse | bytes 8388608 | tf_op jit(solution)/shard_map/jit(rot90)/jit(_flip)/rev | solution.py:24
  178.2 6.6 %rev.46 = f32[64,64,256]{2,1,0:T(8,128)} reverse(f32[64,64,256]{2,1,0:T(8,128)} %bitcast.48), dimensions={0,1} | reverse | bytes 8388608 | tf_op jit(solution)/shard_map/jit(rot90)/jit(_flip)/rev | solution.py:24
  184.9 17.6 %fusion.5 = f32[64,64,256]{2,1,0:T(8,128)} fusion(f32[64,64,256]{2,1,0:T(8,128)} %rev.43, f32[64,64,256]{2,1,0:T(8,128)} %rev.44, f32[64,64,256]{2,0,1:T(8,128)} %bitcast.50, f32[64,64,256]{2,1,0:T(8,128)} %rev.45, f32[64,64,256]{2,1,0:T(8,128)} %rev.46, f32[64,64,256]{2,0,1:T(8,128)} %bitcast.51, f32[64,64,256]{2,1,0:T(8,128)} %bitcast.49, ...), kind=kLoop, calls=%fused_computation.12 | loop fusion | flops 8388608 | bytes 33556480 | tf_op jit(solution)/shard_map/jit(_where)/select_n | solution.py:36
  202.6 9.8 %psum.7 = f32[256]{0:T(256)S(1)} all-reduce(f32[256]{0:T(256)S(1)} %fusion.11), channel_id=1, replica_groups=mesh['groups'=2,'img'=4,'ref'=2,'rep'=2] {'img'}, use_global_device_ids=true, to_apply=%region_8.9 | all-reduce | flops 256 | bytes 2048 | tf_op jit(solution)/shard_map/psum | solution.py:65
  212.4 0.6 broadcast_multiply_fusion
  212.9 64.6 %reduce-scatter.2.cloned.1.call-done = f32[1024,256]{1,0:T(8,128)} async-done(((f32[4096,256]{1,0:T(8,128)}), f32[1024,256]{1,0:T(8,128)}) %reduce-scatter.2.cloned.1.call-update) | async-done | bytes 1048592 | tf_op jit(solution)/shard_map/reduce_scatter | solution.py:76
  277.6 2.3 broadcast_divide_fusion
  (25 shorter events, 1.8 us)
Async XLA Ops:
  7.2 123.5 %copy-start = (f32[96,4096]{1,0:T(8,128)S(1)}, f32[96,4096]{1,0:T(8,128)}, u32[]{:S(2)}) copy-start(f32[96,4096]{1,0:T(8,128)} %param.7) | copy-start | bytes 4718596
  7.2 85.9 %all-gather.4.cloned.1.call-start = ((), (), s32[]{:S(2)}) async-start(), calls=%async_computation.1 | async-start | bytes 5242880 | tf_op jit(solution)/shard_map/all_gather | solution.py:47
  7.9 269.6 %reduce-scatter.2.cloned.1.call-start = ((), (), s32[]{:S(2)}) async-start(), calls=%async_computation.2 | async-start | bytes 5242880 | tf_op jit(solution)/shard_map/reduce_scatter | solution.py:76
  111.0 3.4 %copy-start.1 = (f32[4096,256]{1,0:T(8,128)S(1)}, f32[4096,256]{1,0:T(8,128)}, u32[]{:S(2)}) copy-start(f32[4096,256]{1,0:T(8,128)} %all-gather.4.cloned.1.call-done) | copy-start | bytes 12582916
  140.8 61.7 %copy-start.2 = (f32[96]{0:T(128)}, f32[96]{0:T(128)S(1)}, u32[]{:S(2)}) copy-start(f32[96]{0:T(128)S(1)} %log_add_fusion) | copy-start | bytes 1156
Sparse Core Ops, SparseCore 0:
  9.6 83.4 all-gather.3
  202.6 74.9 reduce-scatter.1
where the time goes:
time: 288 us; the launch traced here: 287 us
  waiting for transfers between devices  147 us (51%)
  local copies, waits for them, and re-layouts  59.2 us (21%)
  other arithmetic  41.3 us (14%)
  blocking collectives  16.3 us (6%)
  between operations  14.8 us (5%)
  matrix products  7.87 us (3%)
    all_gather x1, waiting for transfers between devices, body(): gathered = lax.all_gather(references, 'img', axis=0, tiled=True)  81.7 us
    reduce_scatter x1, waiting for transfers between devices, body(): owned = lax.psum_scatter(numerator, 'img', scatter_dimension=0, tiled=True)  64.6 us
    select_n x2, other arithmetic, select_turn(): jnp.where(rotations[None, None, :] == which, turner(field, which), result)  33.8 us
    rev x4, local copies, waits for them, and re-layouts, turn_forward(): return jnp.rot90(base, quarter, axes=(0, 1))  26.6 us
    rev x3, local copies, waits for them, and re-layouts, turn_inverse(): base = jnp.rot90(field, -quarter, axes=(0, 1))  18 us
    psum x1, blocking collectives, body(): weight_sum = lax.psum(jnp.sum(posterior, axis=0), 'img')  9.77 us
    reshape x1, local copies, waits for them, and re-layouts, body(): numer_image.reshape(IMAGE_SIDE, IMAGE_SIDE, -1)  6.57 us
    unnamed x1, blocking collectives  6.57 us
  transfers between devices with their start and end apart: 2, of which 2 were waited for; matrix products, arithmetic and copies ran while one was open for 1% of the time, Pallas kernels for 0%

commit v1 on v0

--- a/solution.py
+++ b/solution.py
@@ -44,7 +44,9 @@
 
 
 def body(images, references, rotations, image_group, noise_var):
-    gathered = lax.all_gather(references, "img", axis=0, tiled=True)
+    gathered = jnp.concatenate(
+        lax.all_to_all(jnp.stack([references] * lax.axis_size("img")), "img", 0, 0), axis=0
+    )
     rotated = select_turn(
         gathered.reshape(IMAGE_SIDE, IMAGE_SIDE, -1), rotations, turn_inverse
     ).reshape(PIXELS, -1)

time: 288 us -> 314 us (1.090)
  waiting for transfers between devices: 147 us -> 158 us
  local copies, waits for them, and re-layouts: 59.2 us -> 66.2 us
  starting transfers between devices: 0.08 us -> 6.49 us
    all_to_all x0 -> x1, waiting for transfers between devices: none -> 92.1 us  [body(): lax.all_to_all(jnp.stack([references] * lax.axis_size('img')), 'img', 0, 0)]
    all_gather x1 -> x0, waiting for transfers between devices: 81.7 us -> none  [body(): gathered = lax.all_gather(references, 'img', axis=0, tiled=True)]
    another operation x0 -> x2, local copies, waits for them, and re-layouts: none -> 10.2 us  [the longest x1 6.54 us: body(): gathered.reshape(IMAGE_SIDE, IMAGE_SIDE, -1)]
    all_to_all x0 -> x1, starting transfers between devices: none -> 6.49 us  [body(): lax.all_to_all(jnp.stack([references] * lax.axis_size('img')), 'img', 0, 0)]
    select_n x2, other arithmetic: 33.8 us -> 38.2 us  [select_turn(): jnp.where(rotations[None, None, :] == which, turner(field, which), result)]
  transfers between devices with their start and end apart: 2 -> 2, of which waited for: 2 -> 2; matrix products, arithmetic and copies ran while one was open for 1% -> 0% of each run, Pallas kernels for 0% -> 0%
where the time goes in v1:
time: 314 us; the launch traced here: 313 us
  waiting for transfers between devices  158 us (50%)
  local copies, waits for them, and re-layouts  66.2 us (21%)
  other arithmetic  44.2 us (14%)
  blocking collectives  15.7 us (5%)
  between operations  14.8 us (5%)
  matrix products  7.87 us (3%)
  starting transfers between devices  6.49 us (2%)
    all_to_all x1, waiting for transfers between devices, body(): lax.all_to_all(jnp.stack([references] * lax.axis_size('img')), 'img', 0, 0)  92.1 us
    reduce_scatter x1, waiting for transfers between devices, body(): owned = lax.psum_scatter(numerator, 'img', scatter_dimension=0, tiled=True)  65.7 us
    select_n x2, other arithmetic, select_turn(): jnp.where(rotations[None, None, :] == which, turner(field, which), result)  38.2 us
    rev x4, local copies, waits for them, and re-layouts, turn_forward(): return jnp.rot90(base, quarter, axes=(0, 1))  24.6 us
    rev x3, local copies, waits for them, and re-layouts, turn_inverse(): base = jnp.rot90(field, -quarter, axes=(0, 1))  18 us
    psum x1, blocking collectives, body(): weight_sum = lax.psum(jnp.sum(posterior, axis=0), 'img')  9.85 us
    reshape x1, local copies, waits for them, and re-layouts, body(): numer_image.reshape(IMAGE_SIDE, IMAGE_SIDE, -1)  6.57 us
    another operation x1, local copies, waits for them, and re-layouts, body(): gathered.reshape(IMAGE_SIDE, IMAGE_SIDE, -1)  6.54 us
  transfers between devices with their start and end apart: 2, of which 2 were waited for; matrix products, arithmetic and copies ran while one was open for 0% of the time, Pallas kernels for 0%

profile of v1, /device:TPU:0, one launch (start us, length us, event | category | flops | bytes accessed | tf_op | source)
XLA Modules:
  0.0 313.0 jit_solution(15143306080882097010)
XLA Ops:
  7.2 3.6 %stack.2 = f32[4,1024,256]{2,1,0:T(8,128)} broadcast(f32[1024,256]{1,0:T(8,128)} %param.8), dimensions={1,2} | broadcast | bytes 5242880 | tf_op jit(solution)/shard_map/stack | solution.py:48
  10.8 6.5 %all-to-all-start = ((f32[4,1024,256]{2,1,0:T(8,128)}), f32[4,1024,256]{2,1,0:T(8,128)}, u32[]{:S(2)}, u32[]{:S(2)}) async-start(f32[4,1024,256]{2,1,0:T(8,128)} %stack.2), calls=%async_computation | async-start | bytes 8388608 | tf_op jit(solution)/shard_map/all_to_all | solution.py:48
  17.3 0.6 dynamic-slice
  18.7 92.1 %all-to-all-done = f32[4,1024,256]{2,1,0:T(8,128)} async-done(((f32[4,1024,256]{2,1,0:T(8,128)}), f32[4,1024,256]{2,1,0:T(8,128)}, u32[]{:S(2)}, u32[]{:S(2)}) %all-to-all-start) | async-done | bytes 4194336 | tf_op jit(solution)/shard_map/all_to_all | solution.py:48
  110.8 6.7 %rev.40 = f32[64,64,256]{2,1,0:T(8,128)} reverse(f32[64,64,256]{2,1,0:T(8,128)} %bitcast.2), dimensions={1} | reverse | bytes 8388608 | tf_op jit(solution)/shard_map/jit(rot90)/jit(_flip)/rev | solution.py:29
  117.4 6.5 %copy.27 = f32[64,64,256]{2,0,1:T(8,128)} copy(f32[64,64,256]{2,1,0:T(8,128)} %bitcast.2) | data formatting | bytes 8388608 | tf_op jit(solution)/shard_map/reshape;reshape | solution.py:51
  124.0 2.7 multiply_reduce_fusion
  126.7 4.7 %rev.42 = f32[64,64,256]{2,0,1:T(8,128)} reverse(f32[64,64,256]{2,0,1:T(8,128)} %bitcast.4), dimensions={1} | reverse | bytes 8388608 | tf_op jit(solution)/shard_map/jit(rot90)/jit(_flip)/rev | solution.py:29
  131.4 6.6 %rev.41 = f32[64,64,256]{2,0,1:T(8,128)} reverse(f32[64,64,256]{2,0,1:T(8,128)} %copy.27), dimensions={0,1} | reverse | bytes 8388608 | tf_op jit(solution)/shard_map/jit(rot90)/jit(_flip)/rev | solution.py:29
  138.0 20.6 %fusion.9 = f32[64,64,256]{2,1,0:T(8,128)S(1)} fusion(f32[64,64,256]{2,1,0:T(8,128)} %rev.40, f32[64,64,256]{2,0,1:T(8,128)} %rev.42, f32[64,64,256]{2,0,1:T(8,128)} %rev.41, f32[64,64,256]{2,0,1:T(8,128)} %bitcast.4, f32[64,64,256]{2,0,1:T(8,128)} %bitcast.59, f32[64,64,256]{2,1,0:T(8,128)} %bitcast.2, pred[256]{0:T(512)(128)(4,1)S(1)} %get-tuple-element.162, ...), kind=kLoop, calls=%fused_computation.16 | loop fusion | flops 8388608 | bytes 29362176 | tf_op jit(solution)/shard_map/jit(_where)/select_n | solution.py:36
  158.7 2.6 fusion.14
  161.9 5.8 %all-reduce.2 = (f32[384]{0:T(512)S(1)}, f32[384]{0:T(512)S(1)}) all-reduce(f32[384]{0:T(512)S(1)} %dynamic-update-slice, f32[384]{0:T(512)S(1)} %dynamic-update-slice.1), channel_id=2, replica_groups=mesh['groups'=2,'img'=4,'ref'=2,'rep'=2] {'ref','rep'}, use_global_device_ids=true, to_apply=%add | all-reduce | flops 768 | bytes 6144
  168.0 5.3 %convolution_bitcast_fusion = f32[4096,256]{0,1:T(8,128)} fusion(f32[96,4096]{1,0:T(8,128)S(1)} %copy-done, f32[256,96]{0,1:T(8,128)S(1)} %get-tuple-element.165, f32[96]{0:T(128)S(1)} %log_add_fusion), kind=kOutput, calls=%fused_computation.6 | convolution fusion | flops 1207984128 | bytes 5865856 | tf_op jit(solution)/shard_map/dot_general | solution.py:68
  173.3 5.6 %copy.32 = f32[4096,256]{1,0:T(8,128)} copy(f32[4096,256]{0,1:T(8,128)} %convolution_bitcast_fusion) | data formatting | bytes 8388608 | tf_op jit(solution)/shard_map/dot_general | solution.py:68
  178.9 6.6 %copy.54 = f32[64,64,256]{2,0,1:T(8,128)} copy(f32[64,64,256]{2,1,0:T(8,128)} %bitcast.55) | data formatting | bytes 8388608 | tf_op jit(solution)/shard_map/reshape | solution.py:76
  185.5 6.7 %rev.45 = f32[64,64,256]{2,1,0:T(8,128)} reverse(f32[64,64,256]{2,1,0:T(8,128)} %bitcast.53), dimensions={1} | reverse | bytes 8388608 | tf_op jit(solution)/shard_map/jit(rot90)/jit(_flip)/rev | solution.py:24
  192.2 6.6 %rev.44 = f32[64,64,256]{2,1,0:T(8,128)} reverse(f32[64,64,256]{2,1,0:T(8,128)} %bitcast.54), dimensions={0,1} | reverse | bytes 8388608 | tf_op jit(solution)/shard_map/jit(rot90)/jit(_flip)/rev | solution.py:24
  198.8 4.7 %rev.43 = f32[64,64,256]{2,0,1:T(8,128)} reverse(f32[64,64,256]{2,0,1:T(8,128)} %copy.54), dimensions={1} | reverse | bytes 8388608 | tf_op jit(solution)/shard_map/jit(rot90)/jit(_flip)/rev | solution.py:24
  203.5 6.6 %rev.46 = f32[64,64,256]{2,1,0:T(8,128)} reverse(f32[64,64,256]{2,1,0:T(8,128)} %bitcast.56), dimensions={0,1} | reverse | bytes 8388608 | tf_op jit(solution)/shard_map/jit(rot90)/jit(_flip)/rev | solution.py:24
  210.1 17.5 %fusion.7 = f32[64,64,256]{2,1,0:T(8,128)} fusion(f32[64,64,256]{2,1,0:T(8,128)} %rev.44, f32[64,64,256]{2,1,0:T(8,128)} %rev.45, f32[64,64,256]{2,1,0:T(8,128)} %rev.46, f32[64,64,256]{2,0,1:T(8,128)} %rev.43, f32[64,64,256]{2,0,1:T(8,128)} %bitcast.58, f32[64,64,256]{2,1,0:T(8,128)} %bitcast.57, pred[256]{0:T(512)(128)(4,1)S(1)} %get-tuple-element.162, ...), kind=kLoop, calls=%fused_computation.13 | loop fusion | flops 8388608 | bytes 29362176 | tf_op jit(solution)/shard_map/jit(_where)/select_n | solution.py:36
  227.8 9.8 %psum.7 = f32[256]{0:T(256)S(1)} all-reduce(f32[256]{0:T(256)S(1)} %fusion.11), channel_id=1, replica_groups=mesh['groups'=2,'img'=4,'ref'=2,'rep'=2] {'img'}, use_global_device_ids=true, to_apply=%region_8.9 | all-reduce | flops 256 | bytes 2048 | tf_op jit(solution)/shard_map/psum | solution.py:67
  237.6 0.6 broadcast_multiply_fusion
  238.2 65.7 %reduce-scatter.2.cloned.1.call-done = f32[1024,256]{1,0:T(8,128)} async-done(((f32[4096,256]{1,0:T(8,128)}), f32[1024,256]{1,0:T(8,128)}) %reduce-scatter.2.cloned.1.call-update) | async-done | bytes 1048592 | tf_op jit(solution)/shard_map/reduce_scatter | solution.py:78
  303.9 2.3 broadcast_divide_fusion
  (34 shorter events, 1.3 us)
Async XLA Ops:
  7.2 151.5 %copy-start = (f32[96,4096]{1,0:T(8,128)S(1)}, f32[96,4096]{1,0:T(8,128)}, u32[]{:S(2)}) copy-start(f32[96,4096]{1,0:T(8,128)} %param.7) | copy-start | bytes 4718596
  10.8 6.5 %copy-start.6 = (u32[32]{0:T(128)S(1)}, u32[32]{0:T(128)}, u32[]{:S(2)}) copy-start(u32[32]{0:T(128)} %constant.75) | copy-start | bytes 388
  10.8 7.7 %copy-start.4 = (f32[16]{0:T(128)S(1)}, f32[16]{0:T(128)}, u32[]{:S(2)}) copy-start(f32[16]{0:T(128)} %param.11) | copy-start | bytes 196
  10.8 7.7 %copy-start.5 = (s32[96]{0:T(128)S(1)}, s32[96]{0:T(128)}, u32[]{:S(2)}) copy-start(s32[96]{0:T(128)} %param.10) | copy-start | bytes 1156
  10.8 7.8 %copy-start.3 = (s32[256]{0:T(256)S(1)}, s32[256]{0:T(256)}, u32[]{:S(2)}) copy-start(s32[256]{0:T(256)} %param.9) | copy-start | bytes 3076
  10.8 99.9 %all-to-all-start = ((f32[4,1024,256]{2,1,0:T(8,128)}), f32[4,1024,256]{2,1,0:T(8,128)}, u32[]{:S(2)}, u32[]{:S(2)}) async-start(f32[4,1024,256]{2,1,0:T(8,128)} %stack.2), calls=%async_computation | async-start | bytes 8388608 | tf_op jit(solution)/shard_map/all_to_all | solution.py:48
  17.3 286.6 %reduce-scatter.2.cloned.1.call-start = ((), (), s32[]{:S(2)}) async-start(), calls=%async_computation.2 | async-start | bytes 5242880 | tf_op jit(solution)/shard_map/reduce_scatter | solution.py:78
  168.0 59.7 %copy-start.2 = (f32[96]{0:T(128)}, f32[96]{0:T(128)S(1)}, u32[]{:S(2)}) copy-start(f32[96]{0:T(128)S(1)} %log_add_fusion) | copy-start | bytes 1156
  210.1 96.1 %copy-start.1 = (f32[96,4096]{1,0:T(8,128)S(1)}, f32[96,4096]{1,0:T(8,128)}, u32[]{:S(2)}) copy-start(f32[96,4096]{1,0:T(8,128)} %param.7) | copy-start | bytes 4718596
Sparse Core Ops, SparseCore 0:
  227.8 76.0 reduce-scatter.1
